TPU v7x, 32 devices: a whole 2x2x4 slice. The times are simulated.
32 devices in a mesh: dp: 4 (over x, core), expert: 8 (over z, y).
Axes of the slice: x: 2, y: 2, z: 4, core: 2. Of those that a mesh axis runs over, the one named last changes fastest.
Arguments:
- tokens: bfloat16 [4096, 1024], P(('dp', 'expert')), may hold values from -6 to 6
- expert_ids: int32 [4096, 1], P(('dp', 'expert')), may hold values from 0 to 7; in each aligned block of 128 rows (0 to 127, 128 to 255, ...) at most 48 rows name the same one
- gate_scale: float32 [4096], P(('dp', 'expert')), may hold values from 0.1 to 1
- w_gate_up: bfloat16 [8, 1024, 768], P('expert'), may hold values from -0.1875 to 0.1875
- w_down: bfloat16 [8, 1024, 384], P('expert'), may hold values from -0.3125 to 0.3125
- out_grad: bfloat16 [4096, 1024], P(('dp', 'expert')), may hold values from -1.5 to 1.5
Outputs:
- mixed: bfloat16 [4096, 1024], P(('dp', 'expert'))
- input_rows: bfloat16 [4096, 1024], P(('dp', 'expert'))
- gate_grad_rows: float32 [4096], P(('dp', 'expert'))
- grad_gate_up: float32 [8, 1024, 768], P('expert', 'dp')
- grad_down: float32 [8, 1024, 384], P('expert', 'dp')
Inputs may be any that keep to these rules, and one draw needn't show every extreme that they name: `expert_ids`: among the rows of one device no expert is named more than 48 times, a bound that some block reaches.
All inputs are finite; a program needn't handle non-finite values.
Results may differ from a plain program's by a relative error of at most 0.017.
Values may be sent and summed in bfloat16 or wider, within the bound.
A program may use at most 64 MiB of HBM per device.

v0:
```python
import jax
import jax.numpy as jnp
from jax import lax
from jax.sharding import PartitionSpec as P

BLOCK = 128


def slot_places(route_ids, experts, capacity):
    onehot = (route_ids[:, None] == jnp.arange(experts, dtype=jnp.int32)[None, :]).astype(jnp.int32)
    before = jnp.cumsum(onehot, axis=0) - onehot
    position = jnp.sum(before * onehot, axis=1)
    slot_index = route_ids * capacity + position
    return (slot_index[None, :] == jnp.arange(experts * capacity, dtype=jnp.int32)[:, None]).astype(
        jnp.bfloat16
    )


def contract_rows(left, right):
    return lax.dot_general(
        left, right, (((0,), (0,)), ((), ())), preferred_element_type=jnp.float32
    )


def contract_last(left, right):
    return lax.dot_general(
        left, right, (((1,), (1,)), ((), ())), preferred_element_type=jnp.float32
    )


def expert_forward(slot_rows, weight_in, weight_out):
    hidden_units = weight_out.shape[1]
    gate_up = jnp.dot(slot_rows, weight_in, preferred_element_type=jnp.float32)
    gate_part = gate_up[:, :hidden_units]
    up_part = gate_up[:, hidden_units:]
    hidden = (gate_part * jax.nn.sigmoid(gate_part) * up_part).astype(jnp.bfloat16)
    result = contract_last(hidden, weight_out).astype(jnp.bfloat16)
    return (gate_part, up_part, hidden, result)


def expert_backward(slot_grads, gate_part, up_part, weight_in, weight_out):
    hidden_grad = jnp.dot(slot_grads, weight_out, preferred_element_type=jnp.float32)
    sig_gate = jax.nn.sigmoid(gate_part)
    gate_grad = hidden_grad * up_part * sig_gate * (1.0 + gate_part * (1.0 - sig_gate))
    up_grad = hidden_grad * gate_part * sig_gate
    both_grads = jnp.concatenate([gate_grad, up_grad], axis=1).astype(jnp.bfloat16)
    input_grad = contract_last(both_grads, weight_in).astype(jnp.bfloat16)
    return (both_grads, input_grad)


def pick_entry(table, wanted):
    entries = table.shape[-1]
    chosen = (jnp.arange(entries, dtype=jnp.int32) == wanted).astype(jnp.int32)
    return jnp.sum(table * chosen, axis=-1)


def run_blocks(block_source, grad_source, live_rows, weight_in, weight_out):
    length, model_width = block_source.shape
    hidden_units = weight_out.shape[1]
    start_buffers = (
        jnp.zeros((length, model_width), jnp.bfloat16),
        jnp.zeros((length, model_width), jnp.bfloat16),
        jnp.zeros((length, 2 * hidden_units), jnp.bfloat16),
        jnp.zeros((length, hidden_units), jnp.bfloat16),
    )

    def one_block(block_index, buffers):
        first_row = block_index * BLOCK
        block_rows = lax.dynamic_slice_in_dim(block_source, first_row, BLOCK, 0)
        block_grads = lax.dynamic_slice_in_dim(grad_source, first_row, BLOCK, 0)
        gate_part, up_part, hidden, result = expert_forward(block_rows, weight_in, weight_out)
        both_grads, input_grad = expert_backward(
            block_grads, gate_part, up_part, weight_in, weight_out
        )
        fresh = (result, input_grad, both_grads, hidden)
        return tuple(
            (
                lax.dynamic_update_slice_in_dim(buffer, update, first_row, 0)
                for buffer, update in zip(buffers, fresh)
            )
        )

    block_count = (live_rows + BLOCK - 1) // BLOCK
    return lax.fori_loop(0, block_count, one_block, start_buffers)


def on_device(tokens, expert_ids, gate_scale, w_gate_up, w_down, out_grad):
    row_count, model_width = tokens.shape
    experts = lax.axis_size("expert")
    capacity = 3 * row_count // experts
    slot_count = experts * capacity
    spare_rows = slot_count // 4
    length = slot_count + spare_rows + BLOCK
    route = expert_ids[:, 0]
    expert_range = jnp.arange(experts, dtype=jnp.int32)
    counts = jnp.sum((route[:, None] == expert_range[None, :]).astype(jnp.int32), axis=0)
    count_table = lax.all_gather(counts[None, :], "expert", axis=0, tiled=True)
    home = lax.axis_index("expert")
    my_counts = pick_entry(count_table, home)
    loads = jnp.sum(count_table, axis=0)
    my_load = pick_entry(loads, home)
    places = slot_places(route, experts, capacity)
    scaled = (gate_scale[:, None] * out_grad.astype(jnp.float32)).astype(jnp.bfloat16)
    send_rows = jnp.dot(places, tokens, preferred_element_type=jnp.float32).astype(jnp.bfloat16)
    send_grads = jnp.dot(places, scaled, preferred_element_type=jnp.float32).astype(jnp.bfloat16)
    slot_rows, slot_grads = (
        lax.all_to_all(send_rows, "expert", split_axis=0, concat_axis=0, tiled=True),
        lax.all_to_all(send_grads, "expert", split_axis=0, concat_axis=0, tiled=True),
    )
    starts = jnp.cumsum(my_counts) - my_counts
    ends = starts + my_counts
    position = jnp.arange(length, dtype=jnp.int32)
    sender = jnp.sum((ends[None, :] <= position[:, None]).astype(jnp.int32), axis=1)
    sender = jnp.minimum(sender, experts - 1)
    live = position < my_load
    source = jnp.where(
        live, sender * capacity + position - pick_entry(starts[None, :], sender[:, None]), 0
    )
    compact_rows = jnp.where(
        live[:, None], jnp.take(slot_rows, source, axis=0), jnp.zeros((), jnp.bfloat16)
    )
    compact_grads = jnp.where(
        live[:, None], jnp.take(slot_grads, source, axis=0), jnp.zeros((), jnp.bfloat16)
    )
    weight_in = w_gate_up[0]
    weight_out = w_down[0]
    buffers = run_blocks(compact_rows, compact_grads, my_load, weight_in, weight_out)
    result_buffer, ingrad_buffer, both_buffer, hidden_buffer = buffers
    term_width = both_buffer.shape[1] + hidden_buffer.shape[1]
    all_blocks = (my_load + BLOCK - 1) // BLOCK
    slot_index = jnp.arange(slot_count, dtype=jnp.int32)
    slot_sender = slot_index // capacity
    slot_rank = slot_index % capacity
    slot_live = slot_rank < pick_entry(my_counts[None, :], slot_sender[:, None])
    slot_source = jnp.where(
        slot_live, pick_entry(starts[None, :], slot_sender[:, None]) + slot_rank, 0
    )
    back_result = jnp.where(
        slot_live[:, None],
        jnp.take(result_buffer, slot_source, axis=0),
        jnp.zeros((), jnp.bfloat16),
    )
    back_ingrad = jnp.where(
        slot_live[:, None],
        jnp.take(ingrad_buffer, slot_source, axis=0),
        jnp.zeros((), jnp.bfloat16),
    )
    got_result, got_ingrad = (
        lax.all_to_all(back_result, "expert", split_axis=0, concat_axis=0, tiled=True),
        lax.all_to_all(back_ingrad, "expert", split_axis=0, concat_axis=0, tiled=True),
    )

    def add_block(block_index, running):
        first_row = block_index * BLOCK
        rows_part = lax.dynamic_slice(compact_rows, (first_row, 0), (BLOCK, model_width))
        grads_part = lax.dynamic_slice(compact_grads, (first_row, 0), (BLOCK, model_width))
        both_part = lax.dynamic_slice_in_dim(both_buffer, first_row, BLOCK, 0)
        hidden_part = lax.dynamic_slice_in_dim(hidden_buffer, first_row, BLOCK, 0)
        return running + jnp.concatenate(
            [contract_rows(rows_part, both_part), contract_rows(grads_part, hidden_part)], axis=1
        )

    summed = lax.psum_scatter(
        lax.fori_loop(
            0, all_blocks, add_block, jnp.zeros((model_width, term_width), jnp.float32)
        ).astype(jnp.bfloat16),
        "dp",
        scatter_dimension=0,
        tiled=True,
    ).astype(jnp.float32)
    pair_width = weight_in.shape[1]
    ffn_rows = contract_rows(places, got_result)
    mixed = (gate_scale[:, None] * ffn_rows).astype(jnp.bfloat16)
    gate_grad_rows = jnp.sum(out_grad.astype(jnp.float32) * ffn_rows, axis=1)
    input_rows = contract_rows(places, got_ingrad).astype(jnp.bfloat16)
    return (
        mixed,
        input_rows,
        gate_grad_rows,
        summed[:, :pair_width][None],
        summed[:, pair_width:][None],
    )


def solution(mesh):
    return jax.shard_map(
        on_device,
        mesh=mesh,
        in_specs=(
            P(("dp", "expert"), None),
            P(("dp", "expert"), None),
            P(("dp", "expert")),
            P("expert", None, None),
            P("expert", None, None),
            P(("dp", "expert"), None),
        ),
        out_specs=(
            P(("dp", "expert"), None),
            P(("dp", "expert"), None),
            P(("dp", "expert")),
            P("expert", "dp", None),
            P("expert", "dp", None),
        ),
        check_vma=False,
    )
```

profile of v0, /device:TPU:0, one launch (start us, length us, event | category | flops | bytes accessed | tf_op | source)
XLA Modules:
  0.0 186.7 jit_solution(4433873864724181451)
XLA Ops:
  7.2 0.0 copy-start
  7.2 0.8 fusion.27
  8.0 0.2 reduce_window_sum.18
  8.1 0.8 select_reduce_fusion
  9.0 0.7 multiply_add_fusion
  9.6 2.3 %convolution_convert_fusion.2 = bf16[384,1024]{1,0:T(8,128)(2,1)} fusion(bf16[128,1024]{1,0:T(8,128)(2,1)} %param.19, f32[128]{0:T(128)} %param.16, s32[128]{0:T(128)S(1)} %multiply_add_fusion), kind=kOutput, calls=%fused_computation.31 | convolution fusion | flops 101498880 | bytes 1049600 | tf_op jit(solution)/shard_map/dot_general | solution.py:105
  11.9 7.3 %all-to-all-start.1 = ((bf16[8,48,1024]{2,1,0:T(8,128)(2,1)}), bf16[8,48,1024]{2,1,0:T(8,128)(2,1)S(1)}, u32[]{:S(2)}, u32[]{:S(2)}) async-start(bf16[8,48,1024]{2,1,0:T(8,128)(2,1)} %bitcast.8), calls=%async_computation.1 | async-start | bytes 1572864 | tf_op jit(solution)/shard_map/all_to_all | solution.py:108
  19.2 0.0 copy-done
  19.2 0.0 copy-start.11
  19.2 1.2 convolution_convert_fusion.3
  20.5 18.9 %all-to-all-done.1 = bf16[8,48,1024]{2,1,0:T(8,128)(2,1)S(1)} async-done(((bf16[8,48,1024]{2,1,0:T(8,128)(2,1)}), bf16[8,48,1024]{2,1,0:T(8,128)(2,1)S(1)}, u32[]{:S(2)}, u32[]{:S(2)}) %all-to-all-start.1) | async-done | bytes 786464 | tf_op jit(solution)/shard_map/all_to_all | solution.py:108
  39.4 3.6 %all-to-all-start = ((bf16[8,48,1024]{2,1,0:T(8,128)(2,1)}), bf16[8,48,1024]{2,1,0:T(8,128)(2,1)S(1)}, u32[]{:S(2)}, u32[]{:S(2)}) async-start(bf16[8,48,1024]{2,1,0:T(8,128)(2,1)} %bitcast.4), calls=%async_computation | async-start | bytes 1572864 | tf_op jit(solution)/shard_map/all_to_all | solution.py:107
  43.0 0.0 reduce-scatter.2.cloned.1.call-start
  43.0 0.0 copy-done.11
  43.0 0.6 dynamic-slice
  44.3 0.2 dynamic-update-slice
  44.5 19.0 %all-reduce = s32[64]{0:T(128)S(1)} all-reduce(s32[64]{0:T(128)S(1)} %dynamic-update-slice), channel_id=2, replica_groups=mesh['dp'=4,'expert'=8] {'expert'}, use_global_device_ids=true, to_apply=%add | all-reduce | flops 64 | bytes 512
  63.5 0.1 reshape.132
  63.6 0.1 multiply_reduce_fusion
  63.7 0.6 fusion.35
  65.0 0.2 reduce-window.7
  65.2 0.1 convert_reduce_fusion
  65.3 0.1 select_reduce_fusion.1
  65.4 0.7 compare_and_fusion
  66.1 2.9 %gather_fusion.1 = bf16[608,1024]{1,0:T(8,128)(2,1)S(1)} fusion(bf16[384,1024]{1,0:T(8,128)(2,1)S(1)} %bitcast.39, s32[1024]{0:T(1024)S(1)} %pad_clamp_fusion.1), kind=kCustom, calls=%fused_computation.2.clone | custom fusion | bytes 2492800 | tf_op jit(solution)/shard_map/jit(_take)/gather | solution.py:123
  69.0 0.0 all-to-all-done
  69.0 3.5 %gather_fusion = bf16[608,1024]{1,0:T(8,128)(2,1)} fusion(bf16[384,1024]{1,0:T(8,128)(2,1)S(1)} %bitcast.40, s32[1024]{0:T(1024)S(1)} %pad_clamp_fusion.1), kind=kCustom, calls=%fused_computation.clone | custom fusion | bytes 2492800 | tf_op jit(solution)/shard_map/jit(_take)/gather | solution.py:120
  72.5 3.1 %select_select_fusion = (bf16[608,1024]{1,0:T(8,128)(2,1)}, bf16[608,1024]{1,0:T(8,128)(2,1)}) fusion(bf16[608,1024]{1,0:T(8,128)(2,1)S(1)} %gather_fusion.1, pred[608]{0:T(1024)(128)(4,1)S(1)} %get-tuple-element.151, pred[608]{0:T(1024)(128)(4,1)S(1)} %get-tuple-element.161, bf16[608,1024]{1,0:T(8,128)(2,1)} %gather_fusion), kind=kLoop, calls=%fused_computation.33 | loop fusion | flops 2490368 | bytes 4981952 | tf_op jit(solution)/shard_map/jit(_where)/select_n | solution.py:122
  75.6 1.0 broadcast_in_dim.96
  76.6 0.1 broadcast.86.clone
  76.7 1.2 broadcast.86
  77.9 0.4 copy-done.3
  78.3 5.2 %while.26 = (s32[]{:T(128)}, bf16[608,1024]{1,0:T(8,128)(2,1)}, bf16[608,1024]{1,0:T(8,128)(2,1)S(1)}, bf16[608,768]{1,0:T(8,128)(2,1)}, bf16[608,384]{1,0:T(8,1...) while((s32[]{:T(128)}, bf16[608,1024]{1,0:T(8,128)(2,1)}, ...), condition=%wide.region_11.13_spmd, body=%wide.region_10.12_spmd.sunk | while | flops 605962240 | bytes 11174119 | solution.py:84
  78.3 1.4 fusion.67
  79.8 1.3 multiply_convert_fusion.6
  81.0 0.1 constant_dynamic-update-slice_fusion.2
  81.1 0.7 fusion.70
  81.8 0.6 fusion.69
  82.5 1.1 fusion.68
  83.6 2.7 %broadcast_in_dim.101 = f32[1024,1152]{0,1:T(8,128)} broadcast(f32[]{:T(128)} %constant.102.clone.1), dimensions={} | broadcast | bytes 4718596 | tf_op jit(solution)/shard_map/broadcast_in_dim | solution.py:165
  86.3 7.0 %while.27 = (s32[]{:T(128)}, f32[1024,1152]{0,1:T(8,128)}, s32[]{:T(128)}, bf16[608,1024]{1,0:T(8,128)(2,1)}, bf16[608,768]{1,0:T(8,128)(2,1)}, /*index=5*/bf16[...) while((s32[]{:T(128)}, f32[1024,1152]{0,1:T(8,128)}, ...), condition=%wide.region_15.18_spmd, body=%wide.region_14.17_spmd.sunk | while | flops 304349184 | bytes 57444560 | solution.py:164
  86.3 1.5 fusion.75
  87.8 1.6 fusion.76
  89.5 1.7 maximum_add_fusion.2
  91.2 2.1 %copy-done.2 = f32[1024,1152]{0,1:T(8,128)} copy-done((f32[1024,1152]{0,1:T(8,128)}, f32[1024,1152]{0,1:T(8,128)S(1)}, u32[]{:S(2)}) %copy-start.2) | copy-done | bytes 4718616 | tf_op jit(solution)/shard_map/while
  93.3 4.9 %copy.12 = bf16[1024,1152]{1,0:T(8,128)(2,1)} copy(f32[1024,1152]{0,1:T(8,128)} %get-tuple-element.105) | data formatting | bytes 7077888 | tf_op jit(solution)/shard_map/while | solution.py:164
  98.2 0.0 reduce-scatter.2.cloned.1.call-update
  98.3 0.6 copy-done.10
  98.9 0.1 select_reduce_fusion.2
  99.0 0.5 compare_and_fusion.1
  99.5 0.0 copy-done.4
  99.5 2.1 %gather_fusion.2 = bf16[384,1024]{1,0:T(8,128)(2,1)S(1)} fusion(bf16[608,1024]{1,0:T(8,128)(2,1)S(1)} %copy-done.4, s32[1024]{0:T(1024)S(1)} %pad_clamp_fusion), kind=kCustom, calls=%fused_computation.1.clone | custom fusion | bytes 1574400 | tf_op jit(solution)/shard_map/jit(_take)/gather | solution.py:140
  101.6 0.0 copy-start.8
  101.6 2.1 %gather_fusion.3 = bf16[384,1024]{1,0:T(8,128)(2,1)S(1)} fusion(bf16[608,1024]{1,0:T(8,128)(2,1)S(1)} %get-tuple-element.102, s32[1024]{0:T(1024)S(1)} %pad_clamp_fusion), kind=kCustom, calls=%fused_computation.3.clone | custom fusion | bytes 1574400 | tf_op jit(solution)/shard_map/jit(_take)/gather | solution.py:145
  103.7 0.0 copy-done.8
  103.7 1.1 select_select_fusion.2
  104.9 46.8 %all_to_all.48 = bf16[8,48,1024]{2,1,0:T(8,128)(2,1)S(1)} all-to-all(bf16[8,48,1024]{2,1,0:T(8,128)(2,1)S(1)} %bitcast.44), channel_id=1, replica_groups=mesh['dp'=4,'expert'=8] {'expert'}, dimensions={0} | all-to-all | bytes 1572864 | tf_op jit(solution)/shard_map/all_to_all | solution.py:150
  151.7 3.8 %all-to-all-start.2 = ((bf16[8,48,1024]{2,1,0:T(8,128)(2,1)}), bf16[8,48,1024]{2,1,0:T(8,128)(2,1)S(1)}, u32[]{:S(2)}, u32[]{:S(2)}) async-start(bf16[8,48,1024]{2,1,0:T(8,128)(2,1)} %bitcast.10), calls=%async_computation.2 | async-start | bytes 1572864 | tf_op jit(solution)/shard_map/all_to_all | solution.py:149
  155.4 1.1 convolution_convert_fusion.4
  156.5 18.9 %all-to-all-done.2 = bf16[8,48,1024]{2,1,0:T(8,128)(2,1)S(1)} async-done(((bf16[8,48,1024]{2,1,0:T(8,128)(2,1)}), bf16[8,48,1024]{2,1,0:T(8,128)(2,1)S(1)}, u32[]{:S(2)}, u32[]{:S(2)}) %all-to-all-start.2) | async-done | bytes 786464 | tf_op jit(solution)/shard_map/all_to_all | solution.py:149
  175.4 1.7 fusion.19
  177.0 1.1 convert_element_type.64
  178.2 0.8 slice_bitcast_fusion.1
  179.0 0.9 slice_bitcast_fusion
  (23 shorter events, 0.1 us)
Async XLA Ops:
  7.2 12.1 %copy-start = (bf16[128,1024]{1,0:T(8,128)(2,1)S(1)}, bf16[128,1024]{1,0:T(8,128)(2,1)}, u32[]{:S(2)}) copy-start(bf16[128,1024]{1,0:T(8,128)(2,1)} %param.14) | copy-start | bytes 786436
  11.9 27.5 %all-to-all-start.1 = ((bf16[8,48,1024]{2,1,0:T(8,128)(2,1)}), bf16[8,48,1024]{2,1,0:T(8,128)(2,1)S(1)}, u32[]{:S(2)}, u32[]{:S(2)}) async-start(bf16[8,48,1024]{2,1,0:T(8,128)(2,1)} %bitcast.8), calls=%async_computation.1 | async-start | bytes 1572864 | tf_op jit(solution)/shard_map/all_to_all | solution.py:108
  19.2 23.8 %copy-start.11 = (u32[32]{0:T(128)S(1)}, u32[32]{0:T(128)}, u32[]{:S(2)}) copy-start(u32[32]{0:T(128)} %constant.107) | copy-start | bytes 388
  39.4 29.6 %all-to-all-start = ((bf16[8,48,1024]{2,1,0:T(8,128)(2,1)}), bf16[8,48,1024]{2,1,0:T(8,128)(2,1)S(1)}, u32[]{:S(2)}, u32[]{:S(2)}) async-start(bf16[8,48,1024]{2,1,0:T(8,128)(2,1)} %bitcast.4), calls=%async_computation | async-start | bytes 1572864 | tf_op jit(solution)/shard_map/all_to_all | solution.py:107
  43.0 134.1 %reduce-scatter.2.cloned.1.call-start = ((), (), s32[]{:S(2)}) async-start(), calls=%async_computation.5 | async-start | bytes 2949120 | tf_op jit(solution)/shard_map/reduce_scatter | solution.py:163
  63.7 2.4 %copy-start.9 = (s32[8]{0:T(128)}, s32[8]{0:T(128)S(1)}, u32[]{:S(2)}) copy-start(s32[8]{0:T(128)S(1)} %get-tuple-element.106) | copy-start | bytes 100
  76.6 1.8 copy-start.3
  78.3 1.4 copy-start.5
  86.3 3.1 %copy-start.1 = (f32[1024,1152]{0,1:T(8,128)S(1)}, f32[1024,1152]{0,1:T(8,128)}, u32[]{:S(2)}) copy-start(f32[1024,1152]{0,1:T(8,128)} %get-tuple-element.330) | copy-start | bytes 14155780 | tf_op jit(solution)/shard_map/while
  91.2 2.1 %copy-start.2 = (f32[1024,1152]{0,1:T(8,128)}, f32[1024,1152]{0,1:T(8,128)S(1)}, u32[]{:S(2)}) copy-start(f32[1024,1152]{0,1:T(8,128)S(1)} %maximum_add_fusion.2) | copy-start | bytes 14155780 | tf_op jit(solution)/shard_map/while
  98.2 0.7 copy-start.10
  98.2 1.3 copy-start.4
  101.6 2.1 %copy-start.8 = (pred[384]{0:T(512)(128)(4,1)S(1)}, pred[384]{0:T(512)(128)(4,1)}, u32[]{:S(2)}) copy-start(pred[384]{0:T(512)(128)(4,1)} %get-tuple-element.150) | copy-start | bytes 1156
  151.7 23.7 %copy-start.6 = (bf16[128,1024]{1,0:T(8,128)(2,1)S(1)}, bf16[128,1024]{1,0:T(8,128)(2,1)}, u32[]{:S(2)}) copy-start(bf16[128,1024]{1,0:T(8,128)(2,1)} %param.19) | copy-start | bytes 786436
  151.7 23.7 %copy-start.7 = (f32[128]{0:T(128)S(1)}, f32[128]{0:T(128)}, u32[]{:S(2)}) copy-start(f32[128]{0:T(128)} %param.16) | copy-start | bytes 1540
  151.7 23.7 %all-to-all-start.2 = ((bf16[8,48,1024]{2,1,0:T(8,128)(2,1)}), bf16[8,48,1024]{2,1,0:T(8,128)(2,1)S(1)}, u32[]{:S(2)}, u32[]{:S(2)}) async-start(bf16[8,48,1024]{2,1,0:T(8,128)(2,1)} %bitcast.10), calls=%async_computation.2 | async-start | bytes 1572864 | tf_op jit(solution)/shard_map/all_to_all | solution.py:149
Sparse Core Ops, SparseCore 0:
  98.4 54.9 reduce-scatter.1
where the time goes:
time: 186 us; the launch traced here: 187 us
  blocking collectives  65.8 us (35%)
  waiting for transfers between devices  37.8 us (20%)
  local copies, waits for them, and re-layouts  26.4 us (14%)
  between operations  15.5 us (8%)
  starting transfers between devices  14.7 us (8%)
  matrix products  13.7 us (7%)
  other arithmetic  12.7 us (7%)
    all_to_all x1, blocking collectives, on_device(): lax.all_to_all(back_ingrad, 'expert', split_axis=0, concat_axis=0, tiled=...  46.8 us
    unnamed x1, blocking collectives  19 us
    all_to_all x1, waiting for transfers between devices, on_device(): lax.all_to_all(send_grads, 'expert', split_axis=0, concat_axis=0, tiled=T...  18.9 us
    all_to_all x1, waiting for transfers between devices, on_device(): lax.all_to_all(back_result, 'expert', split_axis=0, concat_axis=0, tiled=...  18.9 us
    all_to_all x1, starting transfers between devices, on_device(): lax.all_to_all(send_grads, 'expert', split_axis=0, concat_axis=0, tiled=T...  7.31 us
    dot_general x4, matrix products, contract_rows(): lax.dot_general(left, right, (((0,), (0,)), ((), ())), preferred_element_...  5.84 us
    while x1, local copies, waits for them, and re-layouts, on_device(): lax.fori_loop(0, all_blocks, add_block, jnp.zeros((model_width, term_widt...  4.93 us
    all_to_all x1, starting transfers between devices, on_device(): lax.all_to_all(back_result, 'expert', split_axis=0, concat_axis=0, tiled=...  3.76 us
  transfers between devices with their start and end apart: 4, of which 2 were waited for; matrix products, arithmetic and copies ran while one was open for 8% of the time, Pallas kernels for 0%

commit v1 on v0

v1 whole, which is shorter than its diff:
```python
import functools

import jax
import jax.numpy as jnp
from jax import lax
from jax.experimental import pallas as pl
from jax.experimental.pallas import tpu as pltpu
from jax.sharding import PartitionSpec as P

F32 = jnp.float32
BF16 = jnp.bfloat16
MESH = pl.DeviceIdType.MESH


def dot(left, right):
    return jnp.dot(left, right, preferred_element_type=F32)


def dot_last(left, right):
    return lax.dot_general(left, right, (((1,), (1,)), ((), ())), preferred_element_type=F32)


def dot_rows(left, right):
    return lax.dot_general(left, right, (((0,), (0,)), ((), ())), preferred_element_type=F32)


def flat_rows(value):
    lead, cap, width = value.shape
    if cap % 16:
        return value.astype(F32).reshape(lead * cap, width).astype(BF16)
    return value.reshape(lead * cap, width)


def kernel(
    n, n_dp, cap,
    tokens, ids, gate_row, w_in_hbm, w_out_hbm, out_grad,
    mixed, input_rows, gate_grad, grad_in, grad_out,
    w_in, w_out, sbuf, rbuf, obuf, gbuf, both_buf, hid_buf,
    wacc, wsend1, wrecv1, wsend2, wrecv2,
    w_sem, s_sem, r_sem, os_sem, or_sem, ws1, wr1, ws2, wr2,
):
    rows, width = tokens.shape
    hidden_units = w_out.shape[1]
    slots = n * cap
    me = lax.axis_index("expert")
    dp = lax.axis_index("dp")
    half = n_dp // 2
    core = lax.rem(dp, 2)
    pair = lax.div(dp, 2)
    other = dp + 1 - 2 * core

    copy_in = pltpu.make_async_copy(w_in_hbm.at[0], w_in, w_sem.at[0])
    copy_out = pltpu.make_async_copy(w_out_hbm.at[0], w_out, w_sem.at[1])
    copy_in.start()
    copy_out.start()

    barrier = pltpu.get_barrier_semaphore()
    for k in range(1, n):
        pl.semaphore_signal(barrier, inc=1, device_id={"expert": lax.rem(me + k, n)}, device_id_type=MESH)
    pl.semaphore_signal(barrier, inc=1, device_id={"dp": other}, device_id_type=MESH)
    for j in range(1, half):
        pl.semaphore_signal(barrier, inc=1, device_id={"dp": lax.rem(dp + 2 * j, n_dp)}, device_id_type=MESH)

    lane = lax.broadcasted_iota(jnp.int32, (rows, rows), 1)
    line = lax.broadcasted_iota(jnp.int32, (rows, rows), 0)
    eye = lane == line
    onehot = jnp.where(lane == ids[...], 1.0, 0.0)
    lower = jnp.where(lane < line, 1.0, 0.0).astype(BF16)
    before = dot(lower, onehot.astype(BF16))
    position = jnp.sum(before * onehot, axis=1, keepdims=True)
    slot_col = ids[...].astype(F32) * float(cap) + position
    slot_row = jnp.sum(jnp.where(eye, slot_col, 0.0), axis=0, keepdims=True)
    gate = jnp.sum(jnp.where(eye, gate_row[...], 0.0), axis=1, keepdims=True)
    slot_line = lax.broadcasted_iota(jnp.int32, (slots, rows), 0)
    places = jnp.where(slot_line == slot_row.astype(jnp.int32), 1.0, 0.0).astype(BF16)
    scaled = (gate * out_grad[...].astype(F32)).astype(BF16)
    sbuf[:, :, :width] = dot(places, tokens[...]).reshape(n, cap, width).astype(BF16)
    sbuf[:, :, width:] = dot(places, scaled).reshape(n, cap, width).astype(BF16)
    rbuf[pl.ds(me, 1)] = sbuf[pl.ds(me, 1)]

    pl.semaphore_wait(barrier, n - 1 + half)

    def dispatch(peer):
        return pltpu.make_async_remote_copy(
            src_ref=sbuf.at[peer], dst_ref=rbuf.at[me],
            send_sem=s_sem.at[peer], recv_sem=r_sem.at[me],
            device_id={"expert": peer}, device_id_type=MESH)

    def arrival(peer):
        return pltpu.make_async_remote_copy(
            src_ref=sbuf.at[peer], dst_ref=rbuf.at[peer],
            send_sem=s_sem.at[peer], recv_sem=r_sem.at[peer],
            device_id={"expert": peer}, device_id_type=MESH)

    def give_back(peer):
        return pltpu.make_async_remote_copy(
            src_ref=obuf.at[peer], dst_ref=gbuf.at[me],
            send_sem=os_sem.at[peer], recv_sem=or_sem.at[me],
            device_id={"expert": peer}, device_id_type=MESH)

    def got_back(peer):
        return pltpu.make_async_remote_copy(
            src_ref=obuf.at[peer], dst_ref=gbuf.at[peer],
            send_sem=os_sem.at[peer], recv_sem=or_sem.at[peer],
            device_id={"expert": peer}, device_id_type=MESH)

    def offset(k):
        return lax.rem(jnp.where(lax.rem(k, 2) == 1, (k + 1) // 2, n - k // 2), n)

    for k in range(n - 1, 0, -1):
        off = (k + 1) // 2 if k % 2 else n - k // 2
        dispatch(lax.rem(me + off, n)).start()

    copy_in.wait()
    copy_out.wait()

    def chunk(source, keep):
        block = rbuf[source]
        gate_up = dot(block[:, :width], w_in[...])
        gate_part = gate_up[:, :hidden_units]
        up_part = gate_up[:, hidden_units:]
        sig = jax.nn.sigmoid(gate_part)
        hidden = (gate_part * sig * up_part).astype(BF16)
        hidden_grad = dot(block[:, width:], w_out[...])
        gate_grad_part = hidden_grad * up_part * sig * (1.0 + gate_part * (1.0 - sig))
        up_grad = hidden_grad * gate_part * sig
        both = jnp.concatenate([gate_grad_part, up_grad], axis=1).astype(BF16)
        hid_buf[source] = hidden
        both_buf[source] = both
        keep[source, :, :width] = dot_last(hidden, w_out[...]).astype(BF16)
        keep[source, :, width:] = dot_last(both, w_in[...]).astype(BF16)

    chunk(me, gbuf)

    def one_source(k, carry):
        source = lax.rem(me + offset(k), n)
        arrival(source).wait_recv()
        chunk(source, obuf)
        give_back(source).start()
        return carry

    lax.fori_loop(1, n, one_source, 0)

    both_all = flat_rows(both_buf[...])
    hid_all = flat_rows(hid_buf[...])
    x_all = flat_rows(rbuf[:, :, :width])
    g_all = flat_rows(rbuf[:, :, width:])
    part = width // n_dp
    wacc[:, :, : 2 * hidden_units] = dot_rows(x_all, both_all).reshape(n_dp, part, 2 * hidden_units)
    wacc[:, :, 2 * hidden_units :] = dot_rows(g_all, hid_all).reshape(n_dp, part, hidden_units)

    def pair_copy(j):
        return pltpu.make_async_remote_copy(
            src_ref=wsend1.at[j], dst_ref=wrecv1.at[j],
            send_sem=ws1.at[j], recv_sem=wr1.at[j],
            device_id={"dp": other}, device_id_type=MESH)

    for k in range(half):
        j = lax.rem(pair + 1 + k, half)
        wsend1[j] = wacc[2 * j + 1 - core].astype(BF16)
        pair_copy(j).start()

    def far_copy(j):
        return pltpu.make_async_remote_copy(
            src_ref=wsend2.at[j], dst_ref=wrecv2.at[pair],
            send_sem=ws2.at[j], recv_sem=wr2.at[pair],
            device_id={"dp": 2 * j + core}, device_id_type=MESH)

    def far_arrival(j):
        return pltpu.make_async_remote_copy(
            src_ref=wsend2.at[j], dst_ref=wrecv2.at[j],
            send_sem=ws2.at[j], recv_sem=wr2.at[j],
            device_id={"dp": 2 * j + core}, device_id_type=MESH)

    for k in range(1, half):
        j = lax.rem(pair + k, half)
        pair_copy(j).wait_recv()
        wsend2[j] = (wacc[2 * j + core] + wrecv1[j].astype(F32)).astype(BF16)
        far_copy(j).start()
    pair_copy(pair).wait_recv()
    total = wacc[dp] + wrecv1[pair].astype(F32)
    for k in range(1, half):
        j = lax.rem(pair + k, half)
        far_arrival(j).wait_recv()
        total = total + wrecv2[j].astype(F32)
    grad_in[0] = total[:, : 2 * hidden_units]
    grad_out[0] = total[:, 2 * hidden_units :]

    for k in range(1, n):
        got_back(lax.rem(me + k, n)).wait_recv()
    slot_lane = lax.broadcasted_iota(jnp.int32, (rows, slots), 1)
    picks = jnp.where(slot_lane == slot_col.astype(jnp.int32), 1.0, 0.0).astype(BF16)
    ffn = dot(picks, flat_rows(gbuf[:, :, :width]))
    mixed[...] = (gate * ffn).astype(BF16)
    sums = jnp.sum(out_grad[...].astype(F32) * ffn, axis=1, keepdims=True)
    gate_grad[...] = jnp.sum(jnp.where(eye, sums, 0.0), axis=0, keepdims=True)
    input_rows[...] = dot(picks, flat_rows(gbuf[:, :, width:])).astype(BF16)

    for k in range(1, n):
        peer = lax.rem(me + k, n)
        dispatch(peer).wait_send()
        give_back(peer).wait_send()
    for j in range(half):
        pair_copy(j).wait_send()
    for k in range(1, half):
        far_copy(lax.rem(pair + k, half)).wait_send()


def on_device(n, n_dp, tokens, expert_ids, gate_scale, w_gate_up, w_down, out_grad):
    rows, width = tokens.shape
    hidden_units = w_down.shape[2]
    cap = 3 * rows // n
    part = width // n_dp
    half = n_dp // 2
    terms = 3 * hidden_units
    vmem = pl.BlockSpec(memory_space=pltpu.VMEM)
    anywhere = pl.BlockSpec(memory_space=pl.ANY)
    dma = pltpu.SemaphoreType.DMA
    mixed, input_rows, gate_grad, grad_in, grad_out = pl.pallas_call(
        functools.partial(kernel, n, n_dp, cap),
        out_shape=(
            jax.ShapeDtypeStruct((rows, width), BF16),
            jax.ShapeDtypeStruct((rows, width), BF16),
            jax.ShapeDtypeStruct((1, rows), F32),
            jax.ShapeDtypeStruct((1, part, 2 * hidden_units), F32),
            jax.ShapeDtypeStruct((1, part, hidden_units), F32),
        ),
        in_specs=[vmem, vmem, vmem, anywhere, anywhere, vmem],
        out_specs=(vmem,) * 5,
        scratch_shapes=[
            pltpu.VMEM((width, 2 * hidden_units), BF16),
            pltpu.VMEM((width, hidden_units), BF16),
            pltpu.VMEM((n, cap, 2 * width), BF16),
            pltpu.VMEM((n, cap, 2 * width), BF16),
            pltpu.VMEM((n, cap, 2 * width), BF16),
            pltpu.VMEM((n, cap, 2 * width), BF16),
            pltpu.VMEM((n, cap, 2 * hidden_units), BF16),
            pltpu.VMEM((n, cap, hidden_units), BF16),
            pltpu.VMEM((n_dp, part, terms), F32),
            pltpu.VMEM((half, part, terms), BF16),
            pltpu.VMEM((half, part, terms), BF16),
            pltpu.VMEM((half, part, terms), BF16),
            pltpu.VMEM((half, part, terms), BF16),
            dma((2,)), dma((n,)), dma((n,)), dma((n,)), dma((n,)),
            dma((half,)), dma((half,)), dma((half,)), dma((half,)),
        ],
        compiler_params=pltpu.CompilerParams(
            collective_id=0, has_side_effects=True, vmem_limit_bytes=56 * 1024 * 1024),
    )(tokens, expert_ids, gate_scale[None, :], w_gate_up, w_down, out_grad)
    return mixed, input_rows, gate_grad[0], grad_in, grad_out


def solution(mesh):
    return jax.shard_map(
        functools.partial(on_device, mesh.shape["expert"], mesh.shape["dp"]),
        mesh=mesh,
        in_specs=(
            P(("dp", "expert"), None),
            P(("dp", "expert"), None),
            P(("dp", "expert")),
            P("expert", None, None),
            P("expert", None, None),
            P(("dp", "expert"), None),
        ),
        out_specs=(
            P(("dp", "expert"), None),
            P(("dp", "expert"), None),
            P(("dp", "expert")),
            P("expert", "dp", None),
            P("expert", "dp", None),
        ),
        check_vma=False,
    )
```

time: 186 us -> 87.1 us (0.47)
  Pallas kernels: 0 us -> 78.7 us
  blocking collectives: 65.8 us -> 0 us
  waiting for transfers between devices: 37.8 us -> 0 us
  local copies, waits for them, and re-layouts: 26.4 us -> 7.54 us
  between operations: 15.5 us -> 0.66 us
  starting transfers between devices: 14.7 us -> 0 us
  matrix products: 13.7 us -> 0 us
  other arithmetic: 12.7 us -> 0 us
    pallas_call x0 -> x1, Pallas kernels: none -> 78.7 us  [on_device(): pl.pallas_call(functools.partial(kernel, n, n_dp, cap), out_shape=(jax.Sh...]
    all_to_all x1 -> x0, blocking collectives: 46.8 us -> none  [on_device(): lax.all_to_all(back_ingrad, 'expert', split_axis=0, concat_axis=0, tiled=...]
    all_to_all x3 -> x0, waiting for transfers between devices: 37.8 us -> none  [the longest x1 18.9 us: on_device(): lax.all_to_all(send_grads, 'expert', split_axis=0, concat_axis=0, tiled=T...]
    unnamed x1 -> x0, blocking collectives: 19 us -> none
    all_to_all x3 -> x0, starting transfers between devices: 14.6 us -> none  [the longest x1 7.31 us: on_device(): lax.all_to_all(send_grads, 'expert', split_axis=0, concat_axis=0, tiled=T...]
    dot_general x10 -> x0, matrix products: 13.7 us -> none  [the longest x4 5.84 us: contract_rows(): lax.dot_general(left, right, (((0,), (0,)), ((), ())), preferred_element_...]
    gather x4 -> x0, local copies, waits for them, and re-layouts: 10.5 us -> none  [the longest x1 3.46 us: on_device(): jnp.take(slot_rows, source, axis=0)]
    while x7 -> x0, local copies, waits for them, and re-layouts: 7.08 us -> none  [the longest x1 4.93 us: on_device(): lax.fori_loop(0, all_blocks, add_block, jnp.zeros((model_width, term_widt...]
  transfers between devices with their start and end apart: 4 -> 0, of which waited for: 2 -> 0; matrix products, arithmetic and copies ran while one was open for 8% -> 0% of each run, Pallas kernels for 0% -> 0%
where the time goes in v1:
time: 87.1 us; the launch traced here: 86.9 us
  Pallas kernels  78.7 us (90%)
  local copies, waits for them, and re-layouts  7.54 us (9%)
    pallas_call x1, Pallas kernels, on_device(): pl.pallas_call(functools.partial(kernel, n, n_dp, cap), out_shape=(jax.Sh...  78.7 us
    unnamed x10, local copies, waits for them, and re-layouts  7.54 us

profile of v1, /device:TPU:0, one launch (start us, length us, event | category | flops | bytes accessed | tf_op | source)
XLA Modules:
  0.0 86.9 jit_solution(12992497163327342030)
XLA Ops:
  0.6 1.4 %copy.11.ids = s32[128,1]{1,0:T(8,128)} copy(s32[128,1]{0,1:T(1,128)} %param.7) | data formatting | bytes 1024 | tf_op args[1]
  2.0 78.7 %shard_map.101 = (bf16[128,1024]{1,0:T(8,128)(2,1)}, bf16[128,1024]{1,0:T(8,128)(2,1)}, f32[1,128]{1,0:T(1,128)}, f32[1,256,768]{2,1,0:T(8,128)}, f32[1,256,384]{2,1,0:T(8,128)}) custom-call(bf16[128,1024]{1,0:T(8,128)(2,1)} %tokens.1, s32[128,1]{1,0:T(8,128)} %copy.11.ids, f32[1,128]{1,0:T(1,128)} %bitcast.2, bf16[1,1024,768]{2,1,0:T(8,128)(2,1)} %w_in_hbm.1, ...), custom_call_target="tpu_custom_call" | custom-call | tf_op jit(solution)/shard_map/pallas_call | solution.py:219
  80.7 0.0 copy-start
  80.7 0.0 copy-start.1
  80.7 1.8 %copy.17 = bf16[128,1024]{1,0:T(8,128)(2,1)} copy(bf16[128,1024]{1,0:T(8,128)(2,1)} %get-tuple-element.20) | data formatting | bytes 524288
  82.5 1.7 %copy.18 = bf16[128,1024]{1,0:T(8,128)(2,1)} copy(bf16[128,1024]{1,0:T(8,128)(2,1)} %get-tuple-element.21) | data formatting | bytes 524288
  84.2 1.1 %copy.19 = f32[128]{0:T(128)} copy(f32[128]{0:T(128)} %bitcast.3) | data formatting | bytes 1024
  85.3 0.0 copy-done
  85.3 0.9 %copy.20 = f32[1,256,768]{2,1,0:T(8,128)} copy(f32[1,256,768]{2,1,0:T(8,128)S(1)} %copy-done) | data formatting | bytes 1572864
  86.1 0.0 copy-done.1
  86.1 0.7 copy.21
Async XLA Ops:
  80.7 4.5 %copy-start = (f32[1,256,768]{2,1,0:T(8,128)S(1)}, f32[1,256,768]{2,1,0:T(8,128)}, u32[]{:S(2)}) copy-start(f32[1,256,768]{2,1,0:T(8,128)} %get-tuple-element.23) | copy-start | bytes 2359300
  80.7 5.4 %copy-start.1 = (f32[1,256,384]{2,1,0:T(8,128)S(1)}, f32[1,256,384]{2,1,0:T(8,128)}, u32[]{:S(2)}) copy-start(f32[1,256,384]{2,1,0:T(8,128)} %get-tuple-element.24) | copy-start | bytes 1179652

commit v2 on v1

v2 whole, which is shorter than its diff:
```python
import functools

import jax
import jax.numpy as jnp
from jax import lax
from jax.experimental import pallas as pl
from jax.experimental.pallas import tpu as pltpu
from jax.sharding import PartitionSpec as P

F32 = jnp.float32
BF16 = jnp.bfloat16
MESH = pl.DeviceIdType.MESH


def dot(left, right):
    return jnp.dot(left, right, preferred_element_type=F32)


def dot_last(left, right):
    return lax.dot_general(left, right, (((1,), (1,)), ((), ())), preferred_element_type=F32)


def dot_rows(left, right):
    return lax.dot_general(left, right, (((0,), (0,)), ((), ())), preferred_element_type=F32)


def flat_rows(value):
    lead, cap, width = value.shape
    if cap % 16:
        return value.astype(F32).reshape(lead * cap, width).astype(BF16)
    return value.reshape(lead * cap, width)


def kernel(
    n, n_dp, cap, cuts,
    tokens, ids_row, gate_row, w_in_hbm, w_out_hbm, out_grad,
    mixed, input_rows, gate_grad, grad_in, grad_out,
    w_in, w_out, scaled_buf, info, info_got, raw_got, own_send, far_send, rbuf, obuf,
    own_back, far_back, relay_send, relay_back, gate_up_buf, both_buf, hid_buf,
    wacc, wsend1, wrecv1, wsend2, wrecv2,
    w_sem, is_sem, ir_sem, raw_s, raw_r, own_s, own_r, far_s, far_r,
    ob_s, ob_r, fb_s, fb_r, rb_s, rb_r, ws1, wr1, ws2, wr2,
):
    rows, width = tokens.shape
    hidden_units = w_out.shape[1]
    piece = width // cuts
    h = n // 2
    relays = h // 2
    me = lax.axis_index("expert")
    dp = lax.axis_index("dp")
    half = n_dp // 2
    core = lax.rem(dp, 2)
    pair = lax.div(dp, 2)
    other = dp + 1 - 2 * core
    upper = lax.div(me, h)
    base = upper * h
    mine = me - base
    my_relay = lax.rem(mine, relays)
    my_lane = lax.div(mine, relays)
    relay_start = base + (1 - upper) * relays
    far_relay = (1 - upper) * h + upper * relays + my_relay
    is_relay = lax.div(mine, relays) == 1 - upper
    far_base = (1 - upper) * h

    def remote(source, target, send, receive, peer):
        return pltpu.make_async_remote_copy(
            src_ref=source, dst_ref=target, send_sem=send, recv_sem=receive,
            device_id={"expert": peer}, device_id_type=MESH)

    copy_in = pltpu.make_async_copy(w_in_hbm.at[0], w_in, w_sem.at[0])
    copy_out = pltpu.make_async_copy(w_out_hbm.at[0], w_out, w_sem.at[1])
    copy_in.start()
    copy_out.start()

    barrier = pltpu.get_barrier_semaphore()
    for k in range(1, n):
        pl.semaphore_signal(barrier, inc=1, device_id={"expert": lax.rem(me + k, n)}, device_id_type=MESH)
    pl.semaphore_signal(barrier, inc=1, device_id={"dp": other}, device_id_type=MESH)
    for j in range(1, half):
        pl.semaphore_signal(barrier, inc=1, device_id={"dp": lax.rem(dp + 2 * j, n_dp)}, device_id_type=MESH)

    lane = lax.broadcasted_iota(jnp.int32, (rows, rows), 1)
    line = lax.broadcasted_iota(jnp.int32, (rows, rows), 0)
    eye = lane == line
    ids_f = ids_row[...].astype(F32)
    ids_col = jnp.sum(jnp.where(eye, ids_f, 0.0), axis=1, keepdims=True)
    onehot = jnp.where(lane.astype(F32) == ids_col, 1.0, 0.0)
    lower = jnp.where(lane < line, 1.0, 0.0).astype(BF16)
    before = dot(lower, onehot.astype(BF16))
    position = jnp.sum(before * onehot, axis=1, keepdims=True)
    slot_col = ids_col * float(cap) + position
    slot_row = jnp.sum(jnp.where(eye, slot_col, 0.0), axis=0, keepdims=True)
    info[...] = jnp.broadcast_to(slot_row, info.shape)
    gate = jnp.sum(jnp.where(eye, gate_row[...], 0.0), axis=1, keepdims=True)
    scaled_buf[...] = (gate * out_grad[...].astype(F32)).astype(BF16)

    def place_rows(row):
        spot = lax.broadcasted_iota(jnp.int32, (h * cap, rows), 0) + base * cap
        return jnp.where(spot == row.astype(jnp.int32), 1.0, 0.0).astype(BF16)

    def pick_rows(col):
        spot = lax.broadcasted_iota(jnp.int32, (rows, h * cap), 1) + base * cap
        return jnp.where(spot == col.astype(jnp.int32), 1.0, 0.0).astype(BF16)

    def columns(ref, p):
        q = p % cuts
        return ref.at[:, pl.ds(q * piece, piece)]

    def raw_source(p):
        return columns(tokens if p < cuts else scaled_buf, p)

    def raw_copy(p):
        return remote(raw_source(p), raw_got.at[p, my_lane], raw_s.at[p], raw_r.at[p, my_lane], far_relay)

    def raw_arrival(p, f):
        return remote(raw_source(p), raw_got.at[p, f], raw_s.at[p], raw_r.at[p, f], far_relay)

    def own_copy(p, i):
        return remote(own_send.at[p, i], rbuf.at[p, mine], own_s.at[p, i], own_r.at[p, mine], base + i)

    def own_arrival(p, i):
        return remote(own_send.at[p, i], rbuf.at[p, i], own_s.at[p, i], own_r.at[p, i], base + i)

    def far_copy(p, i):
        return remote(far_send.at[p, i], rbuf.at[p, pl.ds(h + 2 * my_relay, 2)],
                      far_s.at[p, i], far_r.at[p, my_relay], base + i)

    def far_arrival(p, r):
        return remote(far_send.at[p, 0], rbuf.at[p, pl.ds(h + 2 * r, 2)],
                      far_s.at[p, 0], far_r.at[p, r], relay_start + r)

    def own_return(p, i):
        return remote(obuf.at[p, i], own_back.at[p, mine], ob_s.at[p, i], ob_r.at[p, mine], base + i)

    def own_returned(p, i):
        return remote(obuf.at[p, i], own_back.at[p, i], ob_s.at[p, i], ob_r.at[p, i], base + i)

    def far_return(p, r):
        return remote(obuf.at[p, pl.ds(h + 2 * r, 2)], far_back.at[p, mine],
                      fb_s.at[p, r], fb_r.at[p, mine], relay_start + r)

    def far_returned(p, i):
        return remote(obuf.at[p, pl.ds(h, 2)], far_back.at[p, i], fb_s.at[p, 0], fb_r.at[p, i], base + i)

    def relay_copy(p, f):
        return remote(relay_send.at[p, f], relay_back.at[p], rb_s.at[p, f], rb_r.at[p],
                      far_base + f * relays + my_relay)

    def relayed(p):
        return remote(relay_send.at[p, 0], relay_back.at[p], rb_s.at[p, 0], rb_r.at[p], far_relay)

    def info_copy():
        return remote(info, info_got.at[my_lane], is_sem.at[0], ir_sem.at[my_lane], far_relay)

    def info_arrival(f):
        return remote(info, info_got.at[f], is_sem.at[0], ir_sem.at[f], far_relay)

    front, rear = range(cuts), range(cuts, 2 * cuts)
    every = range(2 * cuts)
    own_places = place_rows(slot_row)
    pl.semaphore_wait(barrier, n - 1 + half)
    info_copy().start()
    for part in (front, rear):
        for p in part:
            raw_copy(p).start()
        for p in part:
            own_send[p] = dot(own_places, raw_source(p)[...]).reshape(h, cap, piece).astype(BF16)
            for k in range(1, h):
                own_copy(p, lax.rem(mine + k, h)).start()
            rbuf[p, pl.ds(mine, 1)] = own_send[p, pl.ds(mine, 1)]

    copy_in.wait()
    copy_out.wait()

    def forward(slot, count):
        span = pl.ds(slot, count)
        gate_up = dot(flat_rows(rbuf[0, span]), w_in[:piece])
        for p in front[1:]:
            gate_up += dot(flat_rows(rbuf[p, span]), w_in[p * piece : (p + 1) * piece])
        gate_part = gate_up[:, :hidden_units]
        up_part = gate_up[:, hidden_units:]
        hidden = gate_part * jax.nn.sigmoid(gate_part) * up_part
        gate_up_buf[span] = gate_up.reshape(count, cap, 2 * hidden_units)
        hid_buf[span] = hidden.reshape(count, cap, hidden_units).astype(BF16)
        hidden = hidden.astype(BF16)
        for p in front:
            value = dot_last(hidden, w_out[p * piece : (p + 1) * piece])
            obuf[p, span] = value.reshape(count, cap, piece).astype(BF16)

    def backward(slot, count):
        span = pl.ds(slot, count)
        hidden_grad = dot(flat_rows(rbuf[cuts, span]), w_out[:piece])
        for q in front[1:]:
            hidden_grad += dot(flat_rows(rbuf[cuts + q, span]), w_out[q * piece : (q + 1) * piece])
        gate_up = gate_up_buf[span].reshape(count * cap, 2 * hidden_units)
        gate_part = gate_up[:, :hidden_units]
        up_part = gate_up[:, hidden_units:]
        sig = jax.nn.sigmoid(gate_part)
        gate_term = hidden_grad * up_part * sig * (1.0 + gate_part * (1.0 - sig))
        up_term = hidden_grad * gate_part * sig
        both = jnp.concatenate([gate_term, up_term], axis=1)
        both_buf[span] = both.reshape(count, cap, 2 * hidden_units).astype(BF16)
        both = both.astype(BF16)
        for q in front:
            value = dot_last(both, w_in[q * piece : (q + 1) * piece])
            obuf[cuts + q, span] = value.reshape(count, cap, piece).astype(BF16)

    def own_pass(work, part):
        work(mine, 1)
        for p in part:
            own_back[p, pl.ds(mine, 1)] = obuf[p, pl.ds(mine, 1)]

        def one(k, carry):
            i = lax.rem(mine + k, h)
            for p in part:
                own_arrival(p, i).wait_recv()
            work(i, 1)
            for p in part:
                own_return(p, i).start()
            return carry

        lax.fori_loop(1, h, one, 0)

    def far_pass(work, part):
        def one(k, carry):
            r = lax.rem(my_relay + k, relays)
            myself = jnp.logical_and(is_relay, r == my_relay)

            @pl.when(jnp.logical_not(myself))
            def _():
                for p in part:
                    far_arrival(p, r).wait_recv()

            work(h + 2 * r, 2)

            @pl.when(myself)
            def _():
                for p in part:
                    far_back[p, mine] = obuf[p, pl.ds(h + 2 * r, 2)]

            @pl.when(jnp.logical_not(myself))
            def _():
                for p in part:
                    far_return(p, r).start()

            return carry

        lax.fori_loop(0, relays, one, 0)

    def relay_out(p):
        @pl.when(is_relay)
        def _():
            for f in range(2):
                if p == 0:
                    info_arrival(f).wait_recv()
                raw_arrival(p, f).wait_recv()
                value = dot(place_rows(info_got[f, :1, :]), raw_got[p, f])
                far_send[p, :, f] = value.reshape(h, cap, piece).astype(BF16)
            for k in range(1, h):
                far_copy(p, lax.rem(mine + k, h)).start()
            rbuf[p, pl.ds(h + 2 * my_relay, 2)] = far_send[p, mine]

    def relay_in(part):
        @pl.when(is_relay)
        def _():
            picks = []
            for f in range(2):
                col = jnp.sum(jnp.where(eye, info_got[f, :1, :], 0.0), axis=1, keepdims=True)
                picks.append(pick_rows(col))
            for p in part:
                for k in range(1, h):
                    far_returned(p, lax.rem(mine + k, h)).wait_recv()
                for f in range(2):
                    relay_send[p, f] = dot(picks[f], flat_rows(far_back[p, :, f])).astype(BF16)
                    relay_copy(p, f).start()

    own_pass(forward, front)
    for p in front:
        relay_out(p)
    own_pass(backward, rear)
    for p in rear[:-1]:
        relay_out(p)
    far_pass(forward, front)
    relay_out(rear[-1])
    relay_in(front)
    far_pass(backward, rear)

    both_all = flat_rows(both_buf[...])
    hid_all = flat_rows(hid_buf[...])
    share = width // n_dp
    blocks = n_dp // cuts
    for q in front:
        into = pl.ds(q * blocks, blocks)
        wacc[into, :, : 2 * hidden_units] = dot_rows(flat_rows(rbuf[q]), both_all).reshape(
            blocks, share, 2 * hidden_units)
        wacc[into, :, 2 * hidden_units :] = dot_rows(flat_rows(rbuf[cuts + q]), hid_all).reshape(
            blocks, share, hidden_units)

    def pair_copy(j):
        return pltpu.make_async_remote_copy(
            src_ref=wsend1.at[j], dst_ref=wrecv1.at[j],
            send_sem=ws1.at[j], recv_sem=wr1.at[j],
            device_id={"dp": other}, device_id_type=MESH)

    for k in range(half):
        j = lax.rem(pair + 1 + k, half)
        wsend1[j] = wacc[2 * j + 1 - core].astype(BF16)
        pair_copy(j).start()

    def group_copy(j):
        return pltpu.make_async_remote_copy(
            src_ref=wsend2.at[j], dst_ref=wrecv2.at[pair],
            send_sem=ws2.at[j], recv_sem=wr2.at[pair],
            device_id={"dp": 2 * j + core}, device_id_type=MESH)

    def group_arrival(j):
        return pltpu.make_async_remote_copy(
            src_ref=wsend2.at[j], dst_ref=wrecv2.at[j],
            send_sem=ws2.at[j], recv_sem=wr2.at[j],
            device_id={"dp": 2 * j + core}, device_id_type=MESH)

    for k in range(1, half):
        j = lax.rem(pair + k, half)
        pair_copy(j).wait_recv()
        wsend2[j] = (wacc[2 * j + core] + wrecv1[j].astype(F32)).astype(BF16)
        group_copy(j).start()

    relay_in(rear)

    picks = pick_rows(slot_col)
    for k in range(1, h):
        for p in every:
            own_returned(p, lax.rem(mine + k, h)).wait_recv()
    sums = jnp.zeros((rows, 1), F32)
    for p in front:
        into = pl.ds(p * piece, piece)
        relayed(p).wait_recv()
        ffn = dot(picks, flat_rows(own_back[p])) + relay_back[p].astype(F32)
        mixed[:, into] = (gate * ffn).astype(BF16)
        sums += jnp.sum(out_grad[:, into].astype(F32) * ffn, axis=1, keepdims=True)
    gate_grad[...] = jnp.sum(jnp.where(eye, sums, 0.0), axis=0, keepdims=True)

    pair_copy(pair).wait_recv()
    total = wacc[dp] + wrecv1[pair].astype(F32)
    for k in range(1, half):
        j = lax.rem(pair + k, half)
        group_arrival(j).wait_recv()
        total = total + wrecv2[j].astype(F32)
    grad_in[0] = total[:, : 2 * hidden_units]
    grad_out[0] = total[:, 2 * hidden_units :]

    for q in front:
        p = cuts + q
        relayed(p).wait_recv()
        value = dot(picks, flat_rows(own_back[p])) + relay_back[p].astype(F32)
        input_rows[:, pl.ds(q * piece, piece)] = value.astype(BF16)

    info_copy().wait_send()
    for p in every:
        raw_copy(p).wait_send()
        for k in range(1, h):
            i = lax.rem(mine + k, h)
            own_copy(p, i).wait_send()
            own_return(p, i).wait_send()
        for r in range(relays):
            @pl.when(jnp.logical_not(jnp.logical_and(is_relay, my_relay == r)))
            def _():
                far_return(p, r).wait_send()

    @pl.when(is_relay)
    def _():
        for p in every:
            for k in range(1, h):
                far_copy(p, lax.rem(mine + k, h)).wait_send()
            for f in range(2):
                relay_copy(p, f).wait_send()
    for j in range(half):
        pair_copy(j).wait_send()
    for k in range(1, half):
        group_copy(lax.rem(pair + k, half)).wait_send()


def pass_on(*refs):
    count = len(refs) // 2
    for source, target in zip(refs[:count], refs[count:]):
        target[...] = source[...]


def on_device(n, n_dp, tokens, expert_ids, gate_scale, w_gate_up, w_down, out_grad):
    rows, width = tokens.shape
    hidden_units = w_down.shape[2]
    cap = 3 * rows // n
    share = width // n_dp
    half = n_dp // 2
    terms = 3 * hidden_units
    cuts = 2
    piece = width // cuts
    both = 2 * cuts
    h = n // 2
    relays = h // 2
    vmem = pl.BlockSpec(memory_space=pltpu.VMEM)
    anywhere = pl.BlockSpec(memory_space=pl.ANY)
    dma = pltpu.SemaphoreType.DMA
    shapes = (
        jax.ShapeDtypeStruct((rows, width), BF16),
        jax.ShapeDtypeStruct((rows, width), BF16),
        jax.ShapeDtypeStruct((1, rows), F32),
        jax.ShapeDtypeStruct((1, share, 2 * hidden_units), F32),
        jax.ShapeDtypeStruct((1, share, hidden_units), F32),
    )
    results = pl.pallas_call(
        functools.partial(kernel, n, n_dp, cap, cuts),
        out_shape=shapes,
        in_specs=[vmem, vmem, vmem, anywhere, anywhere, vmem],
        out_specs=(vmem,) * 5,
        scratch_shapes=[
            pltpu.VMEM((width, 2 * hidden_units), BF16),
            pltpu.VMEM((width, hidden_units), BF16),
            pltpu.VMEM((rows, width), BF16),
            pltpu.VMEM((8, rows), F32),
            pltpu.VMEM((2, 8, rows), F32),
            pltpu.VMEM((both, 2, rows, piece), BF16),
            pltpu.VMEM((both, h, cap, piece), BF16),
            pltpu.VMEM((both, h, 2, cap, piece), BF16),
            pltpu.VMEM((both, n, cap, piece), BF16),
            pltpu.VMEM((both, n, cap, piece), BF16),
            pltpu.VMEM((both, h, cap, piece), BF16),
            pltpu.VMEM((both, h, 2, cap, piece), BF16),
            pltpu.VMEM((both, 2, rows, piece), BF16),
            pltpu.VMEM((both, rows, piece), BF16),
            pltpu.VMEM((n, cap, 2 * hidden_units), F32),
            pltpu.VMEM((n, cap, 2 * hidden_units), BF16),
            pltpu.VMEM((n, cap, hidden_units), BF16),
            pltpu.VMEM((n_dp, share, terms), F32),
            pltpu.VMEM((half, share, terms), BF16),
            pltpu.VMEM((half, share, terms), BF16),
            pltpu.VMEM((half, share, terms), BF16),
            pltpu.VMEM((half, share, terms), BF16),
            dma((2,)), dma((1,)), dma((2,)),
            dma((both,)), dma((both, 2)),
            dma((both, h)), dma((both, h)),
            dma((both, h)), dma((both, relays)),
            dma((both, h)), dma((both, h)),
            dma((both, relays)), dma((both, h)),
            dma((both, 2)), dma((both,)),
            dma((half,)), dma((half,)), dma((half,)), dma((half,)),
        ],
        compiler_params=pltpu.CompilerParams(
            collective_id=0, has_side_effects=True, vmem_limit_bytes=48 * 1024 * 1024),
    )(tokens, expert_ids.reshape(1, rows), gate_scale[None, :], w_gate_up, w_down, out_grad)
    mixed, input_rows, gate_grad, grad_in, grad_out = pl.pallas_call(
        pass_on,
        out_shape=shapes,
        in_specs=[vmem] * 5,
        out_specs=(vmem,) * 5,
    )(*results)
    return mixed, input_rows, gate_grad[0], grad_in, grad_out


def solution(mesh):
    return jax.shard_map(
        functools.partial(on_device, mesh.shape["expert"], mesh.shape["dp"]),
        mesh=mesh,
        in_specs=(
            P(("dp", "expert"), None),
            P(("dp", "expert"), None),
            P(("dp", "expert")),
            P("expert", None, None),
            P("expert", None, None),
            P(("dp", "expert"), None),
        ),
        out_specs=(
            P(("dp", "expert"), None),
            P(("dp", "expert"), None),
            P(("dp", "expert")),
            P("expert", "dp", None),
            P("expert", "dp", None),
        ),
        check_vma=False,
    )
```

time: 87.1 us -> 82.7 us (0.949)
  the two profiles are of different devices: /device:TPU:0 before, /device:TPU:9 now
where the time goes in v2:
time: 82.7 us; the launch traced here: 82.4 us
  Pallas kernels  72.5 us (88%)
  local copies, waits for them, and re-layouts  9.26 us (11%)
    pallas_call x1, Pallas kernels, on_device(): pl.pallas_call(functools.partial(kernel, n, n_dp, cap, cuts), out_shape=s...  69.9 us
    unnamed x22, local copies, waits for them, and re-layouts  9.26 us
    pallas_call x1, Pallas kernels, on_device(): pl.pallas_call(pass_on, out_shape=shapes, in_specs=[vmem] * 5, out_specs=...  2.59 us

profile of v2, /device:TPU:9, one launch (start us, length us, event | category | flops | bytes accessed | tf_op | source)
XLA Modules:
  0.0 82.4 jit_solution(7272365750455294331)
XLA Ops:
  0.6 0.0 copy-start
  0.6 1.4 %copy-done = bf16[1,1024,768]{2,1,0:T(8,128)(2,1)S(1)} copy-done((bf16[1,1024,768]{2,1,0:T(8,128)(2,1)S(1)}, bf16[1,1024,768]{2,1,0:T(8,128)(2,1)}, u32[]{:S(2)}) %copy-start) | copy-done | bytes 1572888
  2.0 0.0 copy-start.2
  2.0 1.1 %copy-done.2 = bf16[1,1024,384]{2,1,0:T(8,128)(2,1)S(1)} copy-done((bf16[1,1024,384]{2,1,0:T(8,128)(2,1)S(1)}, bf16[1,1024,384]{2,1,0:T(8,128)(2,1)}, u32[]{:S(2)}) %copy-start.2) | copy-done | bytes 786456
  3.2 0.0 copy-start.6
  3.2 0.9 %copy-done.6 = bf16[128,1024]{1,0:T(8,128)(2,1)S(1)} copy-done((bf16[128,1024]{1,0:T(8,128)(2,1)S(1)}, bf16[128,1024]{1,0:T(8,128)(2,1)}, u32[]{:S(2)}) %copy-start.6) | copy-done | bytes 262168
  4.1 0.0 copy-start.7
  4.1 0.9 %copy-done.7 = bf16[128,1024]{1,0:T(8,128)(2,1)S(1)} copy-done((bf16[128,1024]{1,0:T(8,128)(2,1)S(1)}, bf16[128,1024]{1,0:T(8,128)(2,1)}, u32[]{:S(2)}) %copy-start.7) | copy-done | bytes 262168
  5.1 0.0 copy-start.9
  5.1 0.7 copy-done.9
  5.7 0.0 copy-start.10
  5.7 0.7 copy-done.10
  6.4 69.9 %shard_map.101 = (bf16[128,1024]{1,0:T(8,128)(2,1)S(1)}, bf16[128,1024]{1,0:T(8,128)(2,1)S(1)}, f32[1,128]{1,0:T(1,128)S(1)}, f32[1,256,768]{2,1,0:T(8,128)S(1)}, f32[1,256,384]{2,1,0:T(8,128)S(1)}) custom-call(bf16[128,1024]{1,0:T(8,128)(2,1)S(1)} %copy-done.6, s32[1,128]{1,0:T(1,128)S(1)} %bitcast.3, f32[1,128]{1,0:T(1,128)S(1)} %bitcast.4, ...), custom_call_target="tpu_custom_call" | custom-call | tf_op jit(solution)/shard_map/pallas_call | solution.py:411
  76.3 0.0 copy-start.1
  76.3 0.9 %copy-done.1 = f32[1,256,768]{2,1,0:T(8,128)} copy-done((f32[1,256,768]{2,1,0:T(8,128)}, f32[1,256,768]{2,1,0:T(8,128)S(1)}, u32[]{:S(2)}) %copy-start.1) | copy-done | bytes 786456
  77.2 0.0 copy-start.3
  77.2 0.7 copy-done.3
  77.9 0.0 copy-start.4
  77.9 0.7 copy-done.4
  78.6 0.0 copy-start.5
  78.6 0.7 copy-done.5
  79.3 0.0 copy-start.8
  79.4 0.5 copy-done.8
  79.8 2.6 %shard_map.102 = (bf16[128,1024]{1,0:T(8,128)(2,1)}, bf16[128,1024]{1,0:T(8,128)(2,1)}, f32[1,128]{1,0:T(1,128)}, f32[1,256,768]{2,1,0:T(8,128)}, f32[1,256,384]{2,1,0:T(8,128)}) custom-call(bf16[128,1024]{1,0:T(8,128)(2,1)} %copy-done.4, bf16[128,1024]{1,0:T(8,128)(2,1)} %copy-done.5, f32[1,128]{1,0:T(1,128)} %copy-done.8, f32[1,256,768]{2,1,0:T(8,128)} %copy-done.1, ...), custom_call_target="tpu_custom_call" | custom-call | tf_op jit(solution)/shard_map/pallas_call | solution.py:451
Async XLA Ops:
  0.6 1.4 %copy-start = (bf16[1,1024,768]{2,1,0:T(8,128)(2,1)S(1)}, bf16[1,1024,768]{2,1,0:T(8,128)(2,1)}, u32[]{:S(2)}) copy-start(bf16[1,1024,768]{2,1,0:T(8,128)(2,1)} %w_in_hbm.1) | copy-start | bytes 4718596
  2.0 1.1 %copy-start.2 = (bf16[1,1024,384]{2,1,0:T(8,128)(2,1)S(1)}, bf16[1,1024,384]{2,1,0:T(8,128)(2,1)}, u32[]{:S(2)}) copy-start(bf16[1,1024,384]{2,1,0:T(8,128)(2,1)} %w_out_hbm.1) | copy-start | bytes 2359300
  3.2 0.9 %copy-start.6 = (bf16[128,1024]{1,0:T(8,128)(2,1)S(1)}, bf16[128,1024]{1,0:T(8,128)(2,1)}, u32[]{:S(2)}) copy-start(bf16[128,1024]{1,0:T(8,128)(2,1)} %tokens.1) | copy-start | bytes 786436
  4.1 0.9 %copy-start.7 = (bf16[128,1024]{1,0:T(8,128)(2,1)S(1)}, bf16[128,1024]{1,0:T(8,128)(2,1)}, u32[]{:S(2)}) copy-start(bf16[128,1024]{1,0:T(8,128)(2,1)} %out_grad.1) | copy-start | bytes 786436
  5.1 0.7 copy-start.9
  5.7 0.7 copy-start.10
  76.3 0.9 %copy-start.1 = (f32[1,256,768]{2,1,0:T(8,128)}, f32[1,256,768]{2,1,0:T(8,128)S(1)}, u32[]{:S(2)}) copy-start(f32[1,256,768]{2,1,0:T(8,128)S(1)} %get-tuple-element.18.refs_3_) | copy-start | bytes 2359300
  77.2 0.7 copy-start.3
  77.9 0.7 copy-start.4
  78.6 0.7 copy-start.5
  79.3 0.5 copy-start.8

commit v3 on v2

--- a/solution.py
+++ b/solution.py
@@ -33,9 +33,9 @@
 
 def kernel(
     n, n_dp, cap, cuts,
-    tokens, ids_row, gate_row, w_in_hbm, w_out_hbm, out_grad,
+    tokens_hbm, ids_hbm, gate_hbm, w_in_hbm, w_out_hbm, grad_hbm,
     mixed, input_rows, gate_grad, grad_in, grad_out,
-    w_in, w_out, scaled_buf, info, info_got, raw_got, own_send, far_send, rbuf, obuf,
+    tokens, ids_row, gate_row, out_grad, w_in, w_out, scaled_buf, info, info_got, raw_got, own_send, far_send, rbuf, obuf,
     own_back, far_back, relay_send, relay_back, gate_up_buf, both_buf, hid_buf,
     wacc, wsend1, wrecv1, wsend2, wrecv2,
     w_sem, is_sem, ir_sem, raw_s, raw_r, own_s, own_r, far_s, far_r,
@@ -69,6 +69,13 @@
 
     copy_in = pltpu.make_async_copy(w_in_hbm.at[0], w_in, w_sem.at[0])
     copy_out = pltpu.make_async_copy(w_out_hbm.at[0], w_out, w_sem.at[1])
+    loads = [
+        pltpu.make_async_copy(source, target, w_sem.at[2 + i])
+        for i, (source, target) in enumerate((
+            (ids_hbm, ids_row), (gate_hbm, gate_row), (tokens_hbm, tokens), (grad_hbm, out_grad)))
+    ]
+    for load in loads:
+        load.start()
     copy_in.start()
     copy_out.start()
 
@@ -79,6 +86,8 @@
     for j in range(1, half):
         pl.semaphore_signal(barrier, inc=1, device_id={"dp": lax.rem(dp + 2 * j, n_dp)}, device_id_type=MESH)
 
+    for load in loads:
+        load.wait()
     lane = lax.broadcasted_iota(jnp.int32, (rows, rows), 1)
     line = lax.broadcasted_iota(jnp.int32, (rows, rows), 0)
     eye = lane == line
@@ -411,9 +420,13 @@
     results = pl.pallas_call(
         functools.partial(kernel, n, n_dp, cap, cuts),
         out_shape=shapes,
-        in_specs=[vmem, vmem, vmem, anywhere, anywhere, vmem],
+        in_specs=[anywhere] * 6,
         out_specs=(vmem,) * 5,
         scratch_shapes=[
+            pltpu.VMEM((rows, width), BF16),
+            pltpu.VMEM((1, rows), jnp.int32),
+            pltpu.VMEM((1, rows), F32),
+            pltpu.VMEM((rows, width), BF16),
             pltpu.VMEM((width, 2 * hidden_units), BF16),
             pltpu.VMEM((width, hidden_units), BF16),
             pltpu.VMEM((rows, width), BF16),
@@ -436,7 +449,7 @@
             pltpu.VMEM((half, share, terms), BF16),
             pltpu.VMEM((half, share, terms), BF16),
             pltpu.VMEM((half, share, terms), BF16),
-            dma((2,)), dma((1,)), dma((2,)),
+            dma((6,)), dma((1,)), dma((2,)),
             dma((both,)), dma((both, 2)),
             dma((both, h)), dma((both, h)),
             dma((both, h)), dma((both, relays)),
@@ -446,7 +459,7 @@
             dma((half,)), dma((half,)), dma((half,)), dma((half,)),
         ],
         compiler_params=pltpu.CompilerParams(
-            collective_id=0, has_side_effects=True, vmem_limit_bytes=48 * 1024 * 1024),
+            collective_id=0, has_side_effects=True, vmem_limit_bytes=63 * 1024 * 1024),
     )(tokens, expert_ids.reshape(1, rows), gate_scale[None, :], w_gate_up, w_down, out_grad)
     mixed, input_rows, gate_grad, grad_in, grad_out = pl.pallas_call(
         pass_on,

time: 82.7 us -> 73.9 us (0.89)
  the two profiles are of different devices: /device:TPU:9 before, /device:TPU:0 now
where the time goes in v3:
time: 73.9 us; the launch traced here: 72.5 us
  Pallas kernels  71.9 us (97%)
    pallas_call x1, Pallas kernels, on_device(): pl.pallas_call(functools.partial(kernel, n, n_dp, cap, cuts), out_shape=s...  69.3 us
    pallas_call x1, Pallas kernels, on_device(): pl.pallas_call(pass_on, out_shape=shapes, in_specs=[vmem] * 5, out_specs=...  2.6 us

profile of v3, /device:TPU:0, one launch (start us, length us, event | category | flops | bytes accessed | tf_op | source)
XLA Modules:
  0.0 72.5 jit_solution(12172919767673369650)
XLA Ops:
  0.6 69.3 %shard_map.101 = (bf16[128,1024]{1,0:T(8,128)(2,1)}, bf16[128,1024]{1,0:T(8,128)(2,1)}, f32[1,128]{1,0:T(1,128)}, f32[1,256,768]{2,1,0:T(8,128)}, f32[1,256,384]{2,1,0:T(8,128)}) custom-call(bf16[128,1024]{1,0:T(8,128)(2,1)} %tokens_hbm.1, s32[1,128]{1,0:T(1,128)} %bitcast.3, f32[1,128]{1,0:T(1,128)} %bitcast.4, bf16[1,1024,768]{2,1,0:T(8,128)(2,1)} %w_in_hbm.1, ...), custom_call_target="tpu_custom_call" | custom-call | tf_op jit(solution)/shard_map/pallas_call | solution.py:420
  69.9 2.6 %shard_map.102 = (bf16[128,1024]{1,0:T(8,128)(2,1)}, bf16[128,1024]{1,0:T(8,128)(2,1)}, f32[1,128]{1,0:T(1,128)}, f32[1,256,768]{2,1,0:T(8,128)}, f32[1,256,384]{2,1,0:T(8,128)}) custom-call(bf16[128,1024]{1,0:T(8,128)(2,1)} %get-tuple-element.15.refs_0_, bf16[128,1024]{1,0:T(8,128)(2,1)} %get-tuple-element.16.refs_1_, f32[1,128]{1,0:T(1,128)} %get-tuple-element.17.refs_2_, ...), custom_call_target="tpu_custom_call" | custom-call | tf_op jit(solution)/shard_map/pallas_call | solution.py:464

commit v4 on v3

--- a/solution.py
+++ b/solution.py
@@ -169,14 +169,12 @@
     own_places = place_rows(slot_row)
     pl.semaphore_wait(barrier, n - 1 + half)
     info_copy().start()
-    for part in (front, rear):
-        for p in part:
-            raw_copy(p).start()
-        for p in part:
-            own_send[p] = dot(own_places, raw_source(p)[...]).reshape(h, cap, piece).astype(BF16)
-            for k in range(1, h):
-                own_copy(p, lax.rem(mine + k, h)).start()
-            rbuf[p, pl.ds(mine, 1)] = own_send[p, pl.ds(mine, 1)]
+    for p in every:
+        raw_copy(p).start()
+        own_send[p] = dot(own_places, raw_source(p)[...]).reshape(h, cap, piece).astype(BF16)
+        for k in range(1, h):
+            own_copy(p, lax.rem(mine + k, h)).start()
+        rbuf[p, pl.ds(mine, 1)] = own_send[p, pl.ds(mine, 1)]
 
     copy_in.wait()
     copy_out.wait()
@@ -283,14 +281,15 @@
                     relay_send[p, f] = dot(picks[f], flat_rows(far_back[p, :, f])).astype(BF16)
                     relay_copy(p, f).start()
 
+    relay_out(0)
     own_pass(forward, front)
-    for p in front:
+    for p in front[1:]:
         relay_out(p)
-    own_pass(backward, rear)
     for p in rear[:-1]:
         relay_out(p)
     far_pass(forward, front)
     relay_out(rear[-1])
+    own_pass(backward, rear)
     relay_in(front)
     far_pass(backward, rear)
 

time: 73.9 us -> 70 us (0.947)
  the two profiles are of different devices: /device:TPU:0 before, /device:TPU:28 now
where the time goes in v4:
time: 70 us; the launch traced here: 69.8 us
  Pallas kernels  69.2 us (99%)
    pallas_call x1, Pallas kernels, on_device(): pl.pallas_call(functools.partial(kernel, n, n_dp, cap, cuts), out_shape=s...  66.6 us
    pallas_call x1, Pallas kernels, on_device(): pl.pallas_call(pass_on, out_shape=shapes, in_specs=[vmem] * 5, out_specs=...  2.6 us

profile of v4, /device:TPU:28, one launch (start us, length us, event | category | flops | bytes accessed | tf_op | source)
XLA Modules:
  0.0 69.8 jit_solution(18009847741604561782)
XLA Ops:
  0.6 66.6 %shard_map.101 = (bf16[128,1024]{1,0:T(8,128)(2,1)}, bf16[128,1024]{1,0:T(8,128)(2,1)}, f32[1,128]{1,0:T(1,128)}, f32[1,256,768]{2,1,0:T(8,128)}, f32[1,256,384]{2,1,0:T(8,128)}) custom-call(bf16[128,1024]{1,0:T(8,128)(2,1)} %tokens_hbm.1, s32[1,128]{1,0:T(1,128)} %bitcast.3, f32[1,128]{1,0:T(1,128)} %bitcast.4, bf16[1,1024,768]{2,1,0:T(8,128)(2,1)} %w_in_hbm.1, ...), custom_call_target="tpu_custom_call" | custom-call | tf_op jit(solution)/shard_map/pallas_call | solution.py:419
  67.2 2.6 %shard_map.102 = (bf16[128,1024]{1,0:T(8,128)(2,1)}, bf16[128,1024]{1,0:T(8,128)(2,1)}, f32[1,128]{1,0:T(1,128)}, f32[1,256,768]{2,1,0:T(8,128)}, f32[1,256,384]{2,1,0:T(8,128)}) custom-call(bf16[128,1024]{1,0:T(8,128)(2,1)} %get-tuple-element.15.refs_0_, bf16[128,1024]{1,0:T(8,128)(2,1)} %get-tuple-element.16.refs_1_, f32[1,128]{1,0:T(1,128)} %get-tuple-element.17.refs_2_, ...), custom_call_target="tpu_custom_call" | custom-call | tf_op jit(solution)/shard_map/pallas_call | solution.py:463
